TPU v7x, 32 devices: a whole 2x2x4 slice. The times are simulated.
32 devices in a mesh: rows: 4 (over y, x), cols: 8 (over z, core).
Axes of the slice: x: 2, y: 2, z: 4, core: 2. Of those that a mesh axis runs over, the one named last changes fastest.
Arguments:
- pixels: bfloat16 [128, 256, 768], P('rows', 'cols'), may hold values from -6 to 6
- tissue: int32 [128, 256], P('rows', 'cols'), may hold values 0 or 1
- patch_weight: bfloat16 [768, 1024], replicated, may hold values from -0.21875 to 0.21875
- conv_weight: bfloat16 [9, 32, 1024], replicated, may hold values from -0.375 to 0.375
- kv_weight: bfloat16 [1024, 2048], replicated, may hold values from -0.1875 to 0.1875
- query_weight: bfloat16 [1024, 1024], replicated, may hold values from -0.1875 to 0.1875
- out_weight: bfloat16 [1024, 1024], replicated, may hold values from -0.1875 to 0.1875
- latents: bfloat16 [512, 1024], replicated, may hold values from -240 to 240
Outputs:
- features: bfloat16 [128, 256, 1024], P('rows', 'cols')
- latents_out: bfloat16 [512, 1024], P(('rows', 'cols'))
Inputs may be any that keep to these rules, and one draw needn't show every extreme that they name: 1 marks a patch tile that holds tissue, and at least one tile of the slab holds tissue.
All inputs are finite; a program needn't handle non-finite values. No bound on the sum of `tissue` on one device may be relied on, other than what follows from the above.
Results may differ from a plain program's by a relative error of at most 0.03.
Values may be sent and summed in bfloat16 or wider, within the bound.
A program may use at most 128 MiB of HBM per device.

v0:
```python
import functools

import jax
import jax.numpy as jnp
from jax import lax
from jax.experimental import pallas as pl
from jax.experimental.pallas import tpu as pltpu
from jax.sharding import PartitionSpec as P

HEADS = 16
BLOCK = 256
LANES = 128
PAD = 8
F32 = jnp.float32
BF16 = jnp.bfloat16
LOW = -1e30


def dot(a, b):
    return jnp.dot(a, b, preferred_element_type=F32)


def shifted(cells, axis, step):
    count = lax.axis_size(axis)
    pairs = [(i, i + step) for i in range(count) if 0 <= i + step < count]
    return lax.ppermute(cells, axis, pairs)


def core(
    tile_rows, tile_cols, heads,
    main_ref, top_ref, bottom_ref, side_ref, live_ref, patch_ref, conv_ref, kv_ref, query_ref,
    features_ref, part_ref, stat_ref,
    wide_ref, taps_ref, summed_ref, keys_ref,
):
    tokens = tile_rows * tile_cols
    channels = patch_ref.shape[1]
    group = conv_ref.shape[1]
    rows_ext = tile_rows + 2
    col_ext = tile_cols + PAD
    same = (
        lax.broadcasted_iota(jnp.int32, (BLOCK, BLOCK), 0) // group
        == lax.broadcasted_iota(jnp.int32, (BLOCK, BLOCK), 1) // group
    )
    for block in range(channels // BLOCK):
        lanes = slice(block * BLOCK, (block + 1) * BLOCK)
        patch = patch_ref[:, lanes]
        inner = jnp.concatenate(
            [dot(top_ref[...], patch), dot(main_ref[...], patch), dot(bottom_ref[...], patch)], 0
        )
        side = dot(side_ref[...], patch)
        full = jnp.concatenate(
            [inner.reshape(rows_ext, tile_cols, BLOCK), side.reshape(rows_ext, PAD, BLOCK)], 1
        ).reshape(rows_ext * col_ext, BLOCK)
        for col_shift, amount in ((0, 1), (2, rows_ext * col_ext - 1)):
            moved = pltpu.roll(full, amount, 0).reshape(rows_ext, col_ext, BLOCK)
            moved = moved[:, :tile_cols].reshape(rows_ext * tile_cols, BLOCK)
            wide_ref[:, col_shift * BLOCK : (col_shift + 1) * BLOCK] = moved.astype(BF16)
        wide_ref[:, BLOCK : 2 * BLOCK] = inner.astype(BF16)
        for tap in range(9):
            small = conv_ref[tap, :, lanes]
            tiled = jnp.concatenate([small] * (BLOCK // group), 0)
            row_shift, col_shift = tap // 3, tap % 3
            taps_ref[row_shift, col_shift * BLOCK : (col_shift + 1) * BLOCK, :] = jnp.where(
                same, tiled, jnp.zeros_like(tiled)
            )
        total = wide_ref[tile_cols : tile_cols + tokens, BLOCK : 2 * BLOCK].astype(F32)
        for row_shift in range(3):
            first = row_shift * tile_cols
            total = total + dot(wide_ref[first : first + tokens, :], taps_ref[row_shift])
        summed_ref[:, lanes] = total

    chunk = 128
    inverse = 1.0 / channels

    def normalise(step, _):
        at = pl.ds(pl.multiple_of(step * chunk, chunk), chunk)
        values = summed_ref[at, :]
        centred = values - jnp.sum(values, axis=-1, keepdims=True) * inverse
        variance = jnp.sum(centred * centred, axis=-1, keepdims=True) * inverse
        features_ref[at, :] = (centred * lax.rsqrt(variance + 1e-05)).astype(BF16)
        return 0

    lax.fori_loop(0, tokens // chunk, normalise, 0)

    def project(step, _):
        at = pl.ds(pl.multiple_of(step * BLOCK, BLOCK), BLOCK)
        keys_ref[:, at] = dot(features_ref[...], kv_ref[:, at]).astype(BF16)
        return 0

    lax.fori_loop(0, keys_ref.shape[1] // BLOCK, project, 0)

    latent_count = query_ref.shape[0]
    head_dim = channels // heads
    token_lane = lax.broadcasted_iota(jnp.int32, (tokens, LANES), 1)
    query_lane = lax.broadcasted_iota(jnp.int32, (latent_count, LANES), 1)
    token_low = token_lane < head_dim
    query_low = query_lane < head_dim
    stat_ref[...] = jnp.zeros_like(stat_ref)

    def attend(pair, _):
        at = pl.ds(pl.multiple_of(pair * LANES, LANES), LANES)
        value_at = pl.ds(pl.multiple_of(channels + pair * LANES, LANES), LANES)
        queries = query_ref[:, at]
        keys = keys_ref[:, at]
        values = keys_ref[:, value_at]
        live = live_ref[...]
        bias = (live - 1.0) * (-LOW)
        bias = bias.astype(BF16)
        ones = jnp.ones_like(values)
        results = []
        stats = stat_ref[...]
        for which in range(2):
            query_mine = query_low if which == 0 else jnp.logical_not(query_low)
            token_mine = token_low if which == 0 else jnp.logical_not(token_low)
            spot = head_dim if which == 0 else 0
            marker = (query_lane == spot).astype(F32).astype(BF16)
            query_head = jnp.where(query_mine, queries, marker)
            key_head = jnp.where(token_mine, keys, bias)
            value_head = jnp.where(token_mine, values, ones) * live
            scores = lax.dot_general(
                query_head, key_head, (((1,), (1,)), ((), ())), preferred_element_type=F32
            )
            peak = jnp.max(scores, axis=1, keepdims=True)
            weights = jnp.exp(scores - peak).astype(BF16)
            got = dot(weights, value_head)
            results.append(got)
            head = pair * 2 + which
            total = got[:, spot : spot + 1]
            stats = jnp.where(query_lane == head, peak, stats)
            stats = jnp.where(query_lane == head_dim + head, total, stats)
        stat_ref[...] = stats
        numer = jnp.where(query_low, results[0], results[1])
        denom = jnp.where(query_low, results[1], results[0])
        denom = pltpu.roll(denom, head_dim, 1)
        part_ref[:, at] = jnp.where(denom > 0, numer / jnp.maximum(denom, 1e-30), 0.0).astype(BF16)
        return 0

    lax.fori_loop(0, heads // 2, attend, 0)


def local_work(pixels, top, bottom, side, live, patch_weight, conv_weight, kv_weight, queries):
    tile_rows, tile_cols, patch_in = pixels.shape
    channels = patch_weight.shape[1]
    tokens = tile_rows * tile_cols
    latent_count = queries.shape[0]
    rows_ext = tile_rows + 2
    vmem = pl.BlockSpec(memory_space=pltpu.VMEM)
    return pl.pallas_call(
        functools.partial(core, tile_rows, tile_cols, HEADS),
        out_shape=(
            jax.ShapeDtypeStruct((tokens, channels), BF16),
            jax.ShapeDtypeStruct((latent_count, channels), BF16),
            jax.ShapeDtypeStruct((latent_count, LANES), F32),
        ),
        in_specs=[vmem] * 9,
        out_specs=(vmem, vmem, vmem),
        scratch_shapes=[
            pltpu.VMEM((rows_ext * tile_cols, 3 * BLOCK), BF16),
            pltpu.VMEM((3, 3 * BLOCK, BLOCK), BF16),
            pltpu.VMEM((tokens, channels), F32),
            pltpu.VMEM((tokens, 2 * channels), BF16),
        ],
        compiler_params=pltpu.CompilerParams(vmem_limit_bytes=58 * 1024 * 1024),
        name="local_work",
    )(
        pixels.reshape(tokens, patch_in), top, bottom,
        side.reshape(rows_ext * PAD, patch_in), live, patch_weight, conv_weight, kv_weight, queries,
    )


def shards(pixels, tissue, patch_weight, conv_weight, kv_weight, query_weight, out_weight, latents):
    tile_rows, tile_cols, patch_in = pixels.shape
    channels = patch_weight.shape[1]
    tokens = tile_rows * tile_cols
    head_dim = channels // HEADS
    latent_count = latents.shape[0]
    top = shifted(pixels[-1:], "rows", 1)
    bottom = shifted(pixels[:1], "rows", -1)
    first = jnp.concatenate([top[:, :1], pixels[:, :1], bottom[:, :1]], 0)
    last = jnp.concatenate([top[:, -1:], pixels[:, -1:], bottom[:, -1:]], 0)
    left = shifted(last, "cols", 1)
    right = shifted(first, "cols", -1)
    side = jnp.concatenate(
        [right, jnp.zeros((tile_rows + 2, PAD - 2, patch_in), BF16), jnp.roll(left, -1, 0)], 1
    )
    queries = (dot(latents, query_weight).astype(BF16) * (head_dim ** -0.5)).astype(BF16)
    live = jnp.broadcast_to((tissue.reshape(tokens, 1) > 0).astype(BF16), (tokens, LANES))
    features, part, stat = local_work(
        pixels, top[0], bottom[0], side, live, patch_weight, conv_weight, kv_weight, queries
    )
    devices = lax.axis_size(("rows", "cols"))
    own = latent_count // devices
    swap = functools.partial(
        lax.all_to_all, axis_name=("rows", "cols"), split_axis=1, concat_axis=0, tiled=True
    )
    got = swap(part[None]).reshape(devices, own, HEADS, head_dim).astype(F32)
    stats = swap(stat[None])
    peak = stats[:, :, :HEADS]
    total = stats[:, :, head_dim : head_dim + HEADS]
    factor = jnp.exp(peak - jnp.max(peak, axis=0)[None]) * total
    factor = factor / jnp.sum(factor, axis=0)[None]
    attended = jnp.sum(got * factor[:, :, :, None], axis=0).reshape(own, channels)
    normed = attended * lax.rsqrt(jnp.mean(attended * attended, axis=-1, keepdims=True) + 1e-06)
    latents_out = dot(normed.astype(BF16), out_weight).astype(BF16)
    return (features.reshape(tile_rows, tile_cols, channels), latents_out)


def solution(mesh):
    return jax.shard_map(
        shards,
        mesh=mesh,
        in_specs=(P("rows", "cols", None), P("rows", "cols"), P(), P(), P(), P(), P(), P()),
        out_specs=(P("rows", "cols", None), P(("rows", "cols"), None)),
        check_vma=False,
    )
```

profile of v0, /device:TPU:0, one launch (start us, length us, event | category | flops | bytes accessed | tf_op | source)
XLA Modules:
  0.0 137.5 jit_solution(4513040472957856833)
XLA Ops:
  0.6 0.0 copy-start
  0.6 1.0 fusion.4
  1.6 1.3 collective-permute-start.1
  2.9 5.5 %collective-permute-start = (bf16[1,32,768]{2,1,0:T(8,128)(2,1)S(1)}, bf16[1,32,768]{2,1,0:T(8,128)(2,1)S(1)}, u32[]{:S(2)}, u32[]{:S(2)}) collective-permute-start(bf16[1,32,768]{2,1,0:T(8,128)(2,1)S(1)} %get-tuple-element.11), channel_id=1, source_target_pairs={{0,8},{8,16},{16,24},{1,9},{9,17},{17,25},{2,10},{10,18},{18,26},{... | collective-permute-start | bytes 147464 | tf_op jit(solution)/shard_map/ppermute | solution.py:26
  8.4 1.3 fusion.3
  9.7 0.0 copy-done
  9.7 0.0 copy-start.4
  9.7 3.5 %fusion.query_ref = bf16[512,1024]{1,0:T(8,128)(2,1)} fusion(bf16[512,1024]{1,0:T(8,128)(2,1)} %param.15, bf16[1024,1024]{1,0:T(8,128)(2,1)S(1)} %copy-done), kind=kOutput, calls=%fused_computation.3 | convolution fusion | flops 1074790400 | bytes 4194304 | tf_op jit(solution)/shard_map/dot_general | solution.py:20
  13.2 0.0 copy-done.4
  13.2 0.1 reshape.66
  13.3 0.1 pad.1.clone
  13.4 0.0 collective-permute-done.1
  13.4 0.0 copy-start.2
  13.4 0.0 collective-permute-done
  13.4 0.0 copy-start.3
  13.5 1.5 %collective-permute-start.3 = (bf16[34,1,768]{2,0,1:T(8,128)(2,1)S(1)}, bf16[34,1,768]{2,0,1:T(8,128)(2,1)S(1)}, u32[]{:S(2)}, u32[]{:S(2)}) collective-permute-start(bf16[34,1,768]{2,0,1:T(8,128)(2,1)S(1)} %pad_maximum_fusion.1), channel_id=1, source_target_pairs={{0,1},{1,2},{2,3},{3,4},{4,5},{5,6},{6,7},{8,9},{9,10},{10,11},{11... | collective-permute-start | bytes 156680 | tf_op jit(solution)/shard_map/ppermute | solution.py:26
  15.0 1.3 collective-permute-start.2
  16.3 0.0 collective-permute-done.3
  16.4 0.1 copy.27
  16.5 3.8 %collective-permute-done.2 = bf16[34,1,768]{2,0,1:T(8,128)(2,1)S(1)} collective-permute-done((bf16[34,1,768]{2,0,1:T(8,128)(2,1)S(1)}, bf16[34,1,768]{2,0,1:T(8,128)(2,1)S(1)}, u32[]{:S(2)}, u32[]{:S(2)}) %collective-permute-start.2) | collective-permute-done | bytes 52256 | tf_op jit(solution)/shard_map/ppermute | solution.py:26
  20.3 0.1 copy.26
  20.4 1.0 maximum_bitcast_fusion.side_ref
  21.4 0.9 broadcast_in_dim.9.live_ref
  22.3 0.0 copy-done.2
  22.3 0.0 copy-done.3
  22.3 37.5 %local_work.1 = (bf16[1024,1024]{1,0:T(8,128)(2,1)}, bf16[512,1024]{1,0:T(8,128)(2,1)}, f32[512,128]{1,0:T(8,128)}) custom-call(bf16[1024,768]{1,0:T(8,128)(2,1)} %bitcast.31, bf16[32,768]{1,0:T(8,128)(2,1)} %bitcast.35, bf16[32,768]{1,0:T(8,128)(2,1)} %bitcast.34, bf16[272,768]{1,0:T(8,128)(2,1)} %maximum_bitcast_fusion.side_ref, ...), custom_call_target="tpu_custom_call" | custom-call | tf_op jit(solution)/shard_map/local_work/pallas_call | solution.py:148
  59.8 7.5 %all-to-all-start.1 = ((f32[1,512,128]{2,0,1:T(1,128)}), f32[1,512,128]{2,0,1:T(1,128)S(1)}, u32[]{:S(2)}, u32[]{:S(2)}) async-start(f32[1,512,128]{2,0,1:T(1,128)} %bitcast.33), calls=%async_computation.1 | async-start | bytes 524288 | tf_op jit(solution)/shard_map/all_to_all | solution.py:197
  67.3 4.2 %copy.33 = bf16[1,512,1024]{2,0,1:T(2,128)(2,1)} copy(bf16[1,512,1024]{2,1,0:T(8,128)(2,1)} %bitcast.32) | data formatting | bytes 2097152 | tf_op jit(solution)/shard_map/broadcast_in_dim | solution.py:196
  71.4 0.5 broadcast.40
  72.0 8.0 %reduce.7 = bf16[512,1024]{1,0:T(8,128)(2,1)S(1)} reduce(bf16[512,1,1024]{2,1,0:T(2,128)(2,1)} %bitcast.30, bf16[]{:T(256)} %broadcast.40), dimensions={1}, to_apply=%bitcast.26.reduce_sub_computation | reduce | bytes 2097154
  80.0 1.6 %reshape.69 = bf16[32,2,8192]{2,1,0:T(2,128)(2,1)} reshape(bf16[512,1024]{1,0:T(8,128)(2,1)S(1)} %reduce.7) | data formatting | bytes 2097152
  81.6 0.0 all-to-all-done.1
  81.6 5.9 %all-to-all-start = ((bf16[32,2,8192]{2,1,0:T(2,128)(2,1)}), bf16[32,2,8192]{2,1,0:T(2,128)(2,1)S(1)}, u32[]{:S(2)}, u32[]{:S(2)}) async-start(bf16[32,2,8192]{2,1,0:T(2,128)(2,1)} %reshape.69), calls=%async_computation | async-start | bytes 2097152 | tf_op jit(solution)/shard_map/all_to_all | solution.py:196
  87.5 0.1 fusion.1
  87.7 0.9 broadcast_divide_fusion
  88.5 26.2 %all-to-all-done = bf16[32,2,8192]{2,1,0:T(2,128)(2,1)S(1)} async-done(((bf16[32,2,8192]{2,1,0:T(2,128)(2,1)}), bf16[32,2,8192]{2,1,0:T(2,128)(2,1)S(1)}, u32[]{:S(2)}, u32[]{:S(2)}) %all-to-all-start) | async-done | bytes 1048608 | tf_op jit(solution)/shard_map/all_to_all | solution.py:196
  114.7 3.4 %reshape.70 = bf16[512,1,1024]{2,1,0:T(2,128)(2,1)} reshape(bf16[32,2,8192]{2,1,0:T(2,128)(2,1)S(1)} %all-to-all-done) | data formatting | bytes 2097152
  118.2 9.0 %convert_reduce_fusion = f32[512,1024]{1,0:T(8,128)} fusion(bf16[512,1,1024]{2,1,0:T(2,128)(2,1)} %reshape.70), kind=kLoop, calls=%fused_computation.1 | loop fusion | flops 524288 | bytes 3145728 | tf_op jit(solution)/shard_map/convert_element_type | solution.py:196
  127.2 0.0 copy-start.1
  127.2 4.5 %reshape.67 = f32[32,16,16,64]{3,2,1,0:T(8,128)} reshape(f32[512,1024]{1,0:T(8,128)} %convert_reduce_fusion) | data formatting | bytes 4194304 | tf_op jit(solution)/shard_map/convert_element_type | solution.py:196
  131.7 0.0 copy-done.1
  131.7 2.9 %multiply_reduce_fusion = f32[16,16,64]{2,1,0:T(8,128)S(1)} fusion(f32[32,16,16,64]{3,2,1,0:T(8,128)} %reshape.67, f32[32,16,16]{2,1,0:T(8,128)S(1)} %copy-done.1), kind=kLoop, calls=%fused_computation | loop fusion | flops 1032192 | bytes 2195456 | tf_op jit(solution)/shard_map/reduce_sum | solution.py:202
  134.6 0.2 multiply_reduce_fusion.1
  134.8 0.1 reduce_sum.31
  134.9 2.6 %convolution_convert_fusion.1 = bf16[16,1024]{1,0:T(8,128)(2,1)} fusion(bf16[1024,1024]{1,0:T(8,128)(2,1)} %param.14, f32[16,1024]{1,0:T(8,128)S(1)} %reduce_sum.31, f32[16]{0:T(128)S(1)} %add_rsqrt_fusion), kind=kOutput, calls=%fused_computation.4 | convolution fusion | flops 33603584 | bytes 2195520 | tf_op jit(solution)/shard_map/dot_general | solution.py:20
  (13 shorter events, 0.2 us)
Async XLA Ops:
  0.6 9.1 %copy-start = (bf16[1024,1024]{1,0:T(8,128)(2,1)S(1)}, bf16[1024,1024]{1,0:T(8,128)(2,1)}, u32[]{:S(2)}) copy-start(bf16[1024,1024]{1,0:T(8,128)(2,1)} %param.13) | copy-start | bytes 6291460
  1.6 11.8 %collective-permute-start.1 = (bf16[1,32,768]{2,1,0:T(8,128)(2,1)S(1)}, bf16[1,32,768]{2,1,0:T(8,128)(2,1)S(1)}, u32[]{:S(2)}, u32[]{:S(2)}) collective-permute-start(bf16[1,32,768]{2,1,0:T(8,128)(2,1)S(1)} %get-tuple-element.10), channel_id=1, source_target_pairs={{8,0},{16,8},{24,16},{9,1},{17,9},{25,17},{10,2},{18,10},{26,18},{... | collective-permute-start | bytes 147464 | tf_op jit(solution)/shard_map/ppermute | solution.py:26
  2.9 10.5 %collective-permute-start = (bf16[1,32,768]{2,1,0:T(8,128)(2,1)S(1)}, bf16[1,32,768]{2,1,0:T(8,128)(2,1)S(1)}, u32[]{:S(2)}, u32[]{:S(2)}) collective-permute-start(bf16[1,32,768]{2,1,0:T(8,128)(2,1)S(1)} %get-tuple-element.11), channel_id=1, source_target_pairs={{0,8},{8,16},{16,24},{1,9},{9,17},{17,25},{2,10},{10,18},{18,26},{... | collective-permute-start | bytes 147464 | tf_op jit(solution)/shard_map/ppermute | solution.py:26
  9.7 3.5 %copy-start.4 = (s32[32,32]{1,0:T(8,128)S(1)}, s32[32,32]{1,0:T(8,128)}, u32[]{:S(2)}) copy-start(s32[32,32]{1,0:T(8,128)} %param.9) | copy-start | bytes 12292
  13.4 8.9 %copy-start.2 = (bf16[1,32,768]{2,1,0:T(8,128)(2,1)}, bf16[1,32,768]{2,1,0:T(8,128)(2,1)S(1)}, u32[]{:S(2)}) copy-start(bf16[1,32,768]{2,1,0:T(8,128)(2,1)S(1)} %collective-permute-done.1) | copy-start | bytes 147460
  13.4 8.9 %copy-start.3 = (bf16[1,32,768]{2,1,0:T(8,128)(2,1)}, bf16[1,32,768]{2,1,0:T(8,128)(2,1)S(1)}, u32[]{:S(2)}) copy-start(bf16[1,32,768]{2,1,0:T(8,128)(2,1)S(1)} %collective-permute-done) | copy-start | bytes 147460
  13.5 2.8 %collective-permute-start.3 = (bf16[34,1,768]{2,0,1:T(8,128)(2,1)S(1)}, bf16[34,1,768]{2,0,1:T(8,128)(2,1)S(1)}, u32[]{:S(2)}, u32[]{:S(2)}) collective-permute-start(bf16[34,1,768]{2,0,1:T(8,128)(2,1)S(1)} %pad_maximum_fusion.1), channel_id=1, source_target_pairs={{0,1},{1,2},{2,3},{3,4},{4,5},{5,6},{6,7},{8,9},{9,10},{10,11},{11... | collective-permute-start | bytes 156680 | tf_op jit(solution)/shard_map/ppermute | solution.py:26
  15.0 5.3 %collective-permute-start.2 = (bf16[34,1,768]{2,0,1:T(8,128)(2,1)S(1)}, bf16[34,1,768]{2,0,1:T(8,128)(2,1)S(1)}, u32[]{:S(2)}, u32[]{:S(2)}) collective-permute-start(bf16[34,1,768]{2,0,1:T(8,128)(2,1)S(1)} %pad_maximum_fusion), channel_id=1, source_target_pairs={{1,0},{2,1},{3,2},{4,3},{5,4},{6,5},{7,6},{9,8},{10,9},{11,10},{12... | collective-permute-start | bytes 156680 | tf_op jit(solution)/shard_map/ppermute | solution.py:26
  59.8 21.8 %all-to-all-start.1 = ((f32[1,512,128]{2,0,1:T(1,128)}), f32[1,512,128]{2,0,1:T(1,128)S(1)}, u32[]{:S(2)}, u32[]{:S(2)}) async-start(f32[1,512,128]{2,0,1:T(1,128)} %bitcast.33), calls=%async_computation.1 | async-start | bytes 524288 | tf_op jit(solution)/shard_map/all_to_all | solution.py:197
  81.6 33.1 %all-to-all-start = ((bf16[32,2,8192]{2,1,0:T(2,128)(2,1)}), bf16[32,2,8192]{2,1,0:T(2,128)(2,1)S(1)}, u32[]{:S(2)}, u32[]{:S(2)}) async-start(bf16[32,2,8192]{2,1,0:T(2,128)(2,1)} %reshape.69), calls=%async_computation | async-start | bytes 2097152 | tf_op jit(solution)/shard_map/all_to_all | solution.py:196
  127.2 4.6 %copy-start.1 = (f32[32,16,16]{2,1,0:T(8,128)S(1)}, f32[32,16,16]{2,1,0:T(8,128)}, u32[]{:S(2)}) copy-start(f32[32,16,16]{2,1,0:T(8,128)} %broadcast_divide_fusion) | copy-start | bytes 98308
where the time goes:
time: 138 us
  Pallas kernels  37.5 us (27%)
  waiting for transfers between devices  30.1 us (22%)
  starting transfers between devices  22.9 us (17%)
  other arithmetic  22.2 us (16%)
  local copies, waits for them, and re-layouts  18 us (13%)
  matrix products  6.11 us (4%)
    pallas_call x1, Pallas kernels, local_work(): pl.pallas_call(functools.partial(core, tile_rows, tile_cols, HEADS), out_...  37.5 us
    all_to_all x1, waiting for transfers between devices, shards(): got = swap(part[None]).reshape(devices, own, HEADS, head_dim).astype(F32)  26.2 us
    ppermute x4, starting transfers between devices, shifted(): return lax.ppermute(cells, axis, pairs)  9.54 us
    convert_element_type x1, other arithmetic, shards(): got = swap(part[None]).reshape(devices, own, HEADS, head_dim).astype(F32)  8.97 us
    unnamed x1, other arithmetic  8.03 us
    all_to_all x1, starting transfers between devices, shards(): stats = swap(stat[None])  7.46 us
    dot_general x2, matrix products, dot(): return jnp.dot(a, b, preferred_element_type=F32)  6.11 us
    all_to_all x1, starting transfers between devices, shards(): got = swap(part[None]).reshape(devices, own, HEADS, head_dim).astype(F32)  5.88 us
  transfers between devices with their start and end apart: 6, of which 2 were waited for; matrix products, arithmetic and copies ran while one was open for 15% of the time, Pallas kernels for 0%

commit v1 on v0

--- a/solution.py
+++ b/solution.py
@@ -160,12 +160,176 @@
             pltpu.VMEM((tokens, channels), F32),
             pltpu.VMEM((tokens, 2 * channels), BF16),
         ],
-        compiler_params=pltpu.CompilerParams(vmem_limit_bytes=58 * 1024 * 1024),
+        compiler_params=pltpu.CompilerParams(vmem_limit_bytes=40 * 1024 * 1024),
         name="local_work",
     )(
         pixels.reshape(tokens, patch_in), top, bottom,
         side.reshape(rows_ext * PAD, patch_in), live, patch_weight, conv_weight, kv_weight, queries,
     )
+
+
+MESH = pl.DeviceIdType.MESH
+
+
+def spread(values, heads, head_dim, low):
+    return [
+        jnp.where(low, values[:, 2 * pair : 2 * pair + 1], values[:, 2 * pair + 1 : 2 * pair + 2])
+        for pair in range(heads // 2)
+    ]
+
+
+def blend(parts, stats, heads, head_dim):
+    rows = parts[0].shape[0]
+    lane = lax.broadcasted_iota(jnp.int32, (rows, LANES), 1)
+    low = lane < head_dim
+    peaks = stats
+    totals = [pltpu.roll(stat, LANES - head_dim, 1) for stat in stats]
+    top = functools.reduce(jnp.maximum, peaks)
+    shares = [jnp.exp(peak - top) * total for peak, total in zip(peaks, totals)]
+    whole = functools.reduce(jnp.add, shares)
+    inverse = jnp.where(whole > 0, 1.0 / jnp.maximum(whole, 1e-30), 0.0)
+    columns = [0.0] * (heads // 2)
+    for part, share in zip(parts, shares):
+        factors = spread(share * inverse, heads, head_dim, low)
+        for pair in range(heads // 2):
+            piece = part[:, pair * LANES : (pair + 1) * LANES].astype(F32)
+            columns[pair] = columns[pair] + factors[pair] * piece
+    used = lane < heads
+    stat = jnp.where(used, top, 0.0)
+    stat = jnp.where(lane < head_dim, stat, pltpu.roll(jnp.where(used, whole, 0.0), head_dim, 1))
+    return columns, stat
+
+
+def exchange(
+    heads,
+    part_ref, stat_ref, weight_hbm,
+    out_ref,
+    part_one, stat_one, sum_one, tot_one, part_two, stat_two, sum_two, tot_two,
+    part_three, stat_three, weight_ref, send_sem, recv_sem, load_sem,
+):
+    row_count, half, _, own, channels = part_ref.shape
+    head_dim = channels // heads
+    row = lax.axis_index("rows")
+    col = lax.axis_index("cols")
+    side = lax.rem(col, 2)
+    slot = lax.div(col, 2)
+    load = pltpu.make_async_copy(weight_hbm, weight_ref, load_sem)
+    load.start()
+
+    twin = (row, slot * 2 + (1 - side))
+    row_peers = [(lax.rem(row + step, row_count), col) for step in range(1, row_count)]
+    col_peers = [(row, lax.rem(slot + step, half) * 2 + side) for step in range(1, half)]
+    barrier = pltpu.get_barrier_semaphore()
+    for peer in [twin] + row_peers + col_peers:
+        pl.semaphore_signal(barrier, inc=1, device_id=peer, device_id_type=MESH)
+    pl.semaphore_wait(barrier, 1 + len(row_peers) + len(col_peers))
+
+    def send(source, target, peer, number):
+        copy = pltpu.make_async_remote_copy(
+            src_ref=source, dst_ref=target,
+            send_sem=send_sem.at[number], recv_sem=recv_sem.at[number],
+            device_id=peer, device_id_type=MESH,
+        )
+        copy.start()
+        return copy
+
+    copies = [
+        send(part_ref.at[:, :, 1 - side], part_one, twin, 0),
+        send(stat_ref.at[:, :, 1 - side], stat_one, twin, 1),
+    ]
+    for copy in copies:
+        copy.wait()
+
+    def first(index, _):
+        a, b = lax.div(index, half), lax.rem(index, half)
+        columns, stat = blend(
+            [part_ref[a, b, side], part_one[a, b]], [stat_ref[a, b, side], stat_one[a, b]],
+            heads, head_dim,
+        )
+        for pair, column in enumerate(columns):
+            sum_one[a, b, :, pair * LANES : (pair + 1) * LANES] = column.astype(BF16)
+        tot_one[a, b] = stat
+        return 0
+
+    lax.fori_loop(0, row_count * half, first, 0)
+
+    copies = []
+    for step, peer in enumerate(row_peers):
+        number = 2 + 2 * step
+        copies.append(send(sum_one.at[peer[0]], part_two.at[step], peer, number))
+        copies.append(send(tot_one.at[peer[0]], stat_two.at[step], peer, number + 1))
+    for copy in copies:
+        copy.wait()
+
+    def second(b, _):
+        columns, stat = blend(
+            [sum_one[row, b]] + [part_two[step, b] for step in range(row_count - 1)],
+            [tot_one[row, b]] + [stat_two[step, b] for step in range(row_count - 1)],
+            heads, head_dim,
+        )
+        for pair, column in enumerate(columns):
+            sum_two[b, :, pair * LANES : (pair + 1) * LANES] = column.astype(BF16)
+        tot_two[b] = stat
+        return 0
+
+    lax.fori_loop(0, half, second, 0)
+
+    copies = []
+    for step, peer in enumerate(col_peers):
+        number = 2 * row_count + 2 * step
+        where = lax.rem(slot + step + 1, half)
+        copies.append(send(sum_two.at[where], part_three.at[step], peer, number))
+        copies.append(send(tot_two.at[where], stat_three.at[step], peer, number + 1))
+    for copy in copies:
+        copy.wait()
+    columns, _ = blend(
+        [sum_two[slot]] + [part_three[step] for step in range(half - 1)],
+        [tot_two[slot]] + [stat_three[step] for step in range(half - 1)],
+        heads, head_dim,
+    )
+    attended = jnp.concatenate(columns, 1)
+    mean = jnp.sum(attended * attended, axis=-1, keepdims=True) * (1.0 / channels)
+    normed = (attended * lax.rsqrt(mean + 1e-06)).astype(BF16)
+    load.wait()
+    out_ref[...] = dot(normed, weight_ref[...]).astype(BF16)
+
+
+def combine(part, stat, out_weight):
+    row_count, col_count = lax.axis_size("rows"), lax.axis_size("cols")
+    half = col_count // 2
+    latent_count, channels = part.shape
+    own = latent_count // (row_count * col_count)
+    part = part.reshape(row_count, half, 2, own, channels)
+    stat = stat.reshape(row_count, half, 2, own, LANES)
+    vmem = pl.BlockSpec(memory_space=pltpu.VMEM)
+    copies = 2 + 2 * (row_count - 1) + 2 * (half - 1)
+
+    def pairs(*extent):
+        return [
+            pltpu.VMEM(extent + (own, channels), BF16), pltpu.VMEM(extent + (own, LANES), F32)
+        ]
+
+    return pl.pallas_call(
+        functools.partial(exchange, HEADS),
+        out_shape=jax.ShapeDtypeStruct((own, out_weight.shape[1]), BF16),
+        in_specs=[vmem, vmem, pl.BlockSpec(memory_space=pl.ANY)],
+        out_specs=vmem,
+        scratch_shapes=pairs(row_count, half)
+        + pairs(row_count, half)
+        + pairs(row_count - 1, half)
+        + pairs(half)
+        + pairs(half - 1)
+        + [
+            pltpu.VMEM(out_weight.shape, BF16),
+            pltpu.SemaphoreType.DMA((copies,)),
+            pltpu.SemaphoreType.DMA((copies,)),
+            pltpu.SemaphoreType.DMA,
+        ],
+        compiler_params=pltpu.CompilerParams(
+            collective_id=1, has_side_effects=True, vmem_limit_bytes=24 * 1024 * 1024
+        ),
+        name="combine",
+    )(part, stat, out_weight)
 
 
 def shards(pixels, tissue, patch_weight, conv_weight, kv_weight, query_weight, out_weight, latents):
@@ -188,20 +352,7 @@
     features, part, stat = local_work(
         pixels, top[0], bottom[0], side, live, patch_weight, conv_weight, kv_weight, queries
     )
-    devices = lax.axis_size(("rows", "cols"))
-    own = latent_count // devices
-    swap = functools.partial(
-        lax.all_to_all, axis_name=("rows", "cols"), split_axis=1, concat_axis=0, tiled=True
-    )
-    got = swap(part[None]).reshape(devices, own, HEADS, head_dim).astype(F32)
-    stats = swap(stat[None])
-    peak = stats[:, :, :HEADS]
-    total = stats[:, :, head_dim : head_dim + HEADS]
-    factor = jnp.exp(peak - jnp.max(peak, axis=0)[None]) * total
-    factor = factor / jnp.sum(factor, axis=0)[None]
-    attended = jnp.sum(got * factor[:, :, :, None], axis=0).reshape(own, channels)
-    normed = attended * lax.rsqrt(jnp.mean(attended * attended, axis=-1, keepdims=True) + 1e-06)
-    latents_out = dot(normed.astype(BF16), out_weight).astype(BF16)
+    latents_out = combine(part, stat, out_weight)
     return (features.reshape(tile_rows, tile_cols, channels), latents_out)
 
 

time: 138 us -> 88.8 us (0.64)
  waiting for transfers between devices: 30.1 us -> 3.85 us
  Pallas kernels: 37.5 us -> 63.1 us
  other arithmetic: 22.2 us -> 0.33 us
  starting transfers between devices: 22.9 us -> 9.67 us
  local copies, waits for them, and re-layouts: 18 us -> 8.13 us
  matrix products: 6.11 us -> 2.48 us
    pallas_call x0 -> x1, Pallas kernels: none -> 29.2 us  [combine(): pl.pallas_call(functools.partial(exchange, HEADS), out_shape=jax.ShapeDty...]
    all_to_all x2 -> x0, waiting for transfers between devices: 26.2 us -> none  [the longest x1 26.2 us: shards(): got = swap(part[None]).reshape(devices, own, HEADS, head_dim).astype(F32)]
    all_to_all x2 -> x0, starting transfers between devices: 13.3 us -> none  [the longest x1 7.46 us: shards(): stats = swap(stat[None])]
    convert_element_type x1 -> x0, other arithmetic: 8.97 us -> none  [shards(): got = swap(part[None]).reshape(devices, own, HEADS, head_dim).astype(F32)]
    unnamed x1 -> x0, other arithmetic: 8.03 us -> none
    convert_element_type x1 -> x0, local copies, waits for them, and re-layouts: 4.55 us -> none  [shards(): got = swap(part[None]).reshape(devices, own, HEADS, head_dim).astype(F32)]
    broadcast_in_dim x1 -> x0, local copies, waits for them, and re-layouts: 4.19 us -> none  [shards(): got = swap(part[None]).reshape(devices, own, HEADS, head_dim).astype(F32)]
    dot_general x2 -> x1, matrix products: 6.11 us -> 2.48 us  [dot(): return jnp.dot(a, b, preferred_element_type=F32)]
  transfers between devices with their start and end apart: 6 -> 4, of which waited for: 2 -> 1; matrix products, arithmetic and copies ran while one was open for 15% -> 5% of each run, Pallas kernels for 0% -> 0%
where the time goes in v1:
time: 88.8 us; the launch traced here: 88.4 us
  Pallas kernels  63.1 us (71%)
  starting transfers between devices  9.67 us (11%)
  local copies, waits for them, and re-layouts  8.13 us (9%)
  waiting for transfers between devices  3.85 us (4%)
  matrix products  2.48 us (3%)
    pallas_call x1, Pallas kernels, local_work(): pl.pallas_call(functools.partial(core, tile_rows, tile_cols, HEADS), out_...  33.9 us
    pallas_call x1, Pallas kernels, combine(): pl.pallas_call(functools.partial(exchange, HEADS), out_shape=jax.ShapeDty...  29.2 us
    ppermute x4, starting transfers between devices, shifted(): return lax.ppermute(cells, axis, pairs)  9.67 us
    unnamed x17, local copies, waits for them, and re-layouts  5.31 us
    ppermute x4, waiting for transfers between devices, shifted(): return lax.ppermute(cells, axis, pairs)  3.85 us
    dot_general x1, matrix products, dot(): return jnp.dot(a, b, preferred_element_type=F32)  2.48 us
  transfers between devices with their start and end apart: 4, of which 1 were waited for; matrix products, arithmetic and copies ran while one was open for 5% of the time, Pallas kernels for 0%

profile of v1, /device:TPU:0, one launch (start us, length us, event | category | flops | bytes accessed | tf_op | source)
XLA Modules:
  0.0 88.4 jit_solution(636882124021302673)
XLA Ops:
  0.6 0.0 copy-start
  0.6 1.0 %fusion.2 = (bf16[1,32,768]{2,1,0:T(8,128)(2,1)S(1)}, bf16[1,32,768]{2,1,0:T(8,128)(2,1)S(1)}) fusion(bf16[32,32,768]{2,1,0:T(8,128)(2,1)} %param.8), kind=kLoop, calls=%fused_computation.12 | loop fusion | bytes 196608 | tf_op jit(solution)/shard_map/slice | solution.py:342
  1.6 1.3 %collective-permute-start.1 = (bf16[1,32,768]{2,1,0:T(8,128)(2,1)S(1)}, bf16[1,32,768]{2,1,0:T(8,128)(2,1)S(1)}, u32[]{:S(2)}, u32[]{:S(2)}) collective-permute-start(bf16[1,32,768]{2,1,0:T(8,128)(2,1)S(1)} %get-tuple-element.10), channel_id=1, source_target_pairs={{8,0},{16,8},{24,16},{9,1},{17,9},{25,17},{10,2},{18,10},{26,18},{... | collective-permute-start | bytes 147464 | tf_op jit(solution)/shard_map/ppermute | solution.py:26
  2.9 5.5 %collective-permute-start = (bf16[1,32,768]{2,1,0:T(8,128)(2,1)S(1)}, bf16[1,32,768]{2,1,0:T(8,128)(2,1)S(1)}, u32[]{:S(2)}, u32[]{:S(2)}) collective-permute-start(bf16[1,32,768]{2,1,0:T(8,128)(2,1)S(1)} %get-tuple-element.11), channel_id=1, source_target_pairs={{0,8},{8,16},{16,24},{1,9},{9,17},{17,25},{2,10},{10,18},{18,26},{... | collective-permute-start | bytes 147464 | tf_op jit(solution)/shard_map/ppermute | solution.py:26
  8.4 1.3 %fusion.1 = (bf16[32,1,768]{2,1,0:T(2,128)(2,1)S(1)}, bf16[32,1,768]{2,1,0:T(2,128)(2,1)S(1)}) fusion(bf16[32,32,768]{2,1,0:T(8,128)(2,1)} %param.8), kind=kLoop, calls=%fused_computation.11 | loop fusion | bytes 196608 | tf_op jit(solution)/shard_map/slice | solution.py:343
  9.7 0.0 copy-done
  9.7 0.0 copy-start.6
  9.7 2.5 %fusion.query_ref = bf16[512,1024]{1,0:T(8,128)(2,1)S(1)} fusion(bf16[512,1024]{1,0:T(8,128)(2,1)} %param.15, bf16[1024,1024]{1,0:T(8,128)(2,1)S(1)} %copy-done), kind=kOutput, calls=%fused_computation.1 | convolution fusion | flops 1074790400 | bytes 4194304 | tf_op jit(solution)/shard_map/dot_general | solution.py:20
  12.2 0.0 copy-done.6
  12.2 0.1 reshape.38
  12.3 0.0 copy-start.2
  12.4 0.1 pad.1.clone
  12.4 0.0 collective-permute-done.1
  12.5 0.0 collective-permute-done
  12.5 1.6 %collective-permute-start.3 = (bf16[34,1,768]{2,0,1:T(8,128)(2,1)S(1)}, bf16[34,1,768]{2,0,1:T(8,128)(2,1)S(1)}, u32[]{:S(2)}, u32[]{:S(2)}) collective-permute-start(bf16[34,1,768]{2,0,1:T(8,128)(2,1)S(1)} %pad_maximum_fusion.1), channel_id=1, source_target_pairs={{0,1},{1,2},{2,3},{3,4},{4,5},{5,6},{6,7},{8,9},{9,10},{10,11},{11... | collective-permute-start | bytes 156680 | tf_op jit(solution)/shard_map/ppermute | solution.py:26
  14.2 1.3 %collective-permute-start.2 = (bf16[34,1,768]{2,0,1:T(8,128)(2,1)S(1)}, bf16[34,1,768]{2,0,1:T(8,128)(2,1)S(1)}, u32[]{:S(2)}, u32[]{:S(2)}) collective-permute-start(bf16[34,1,768]{2,0,1:T(8,128)(2,1)S(1)} %pad_maximum_fusion), channel_id=1, source_target_pairs={{1,0},{2,1},{3,2},{4,3},{5,4},{6,5},{7,6},{9,8},{10,9},{11,10},{12... | collective-permute-start | bytes 156680 | tf_op jit(solution)/shard_map/ppermute | solution.py:26
  15.5 0.0 collective-permute-done.3
  15.5 0.1 copy.17
  15.6 3.8 %collective-permute-done.2 = bf16[34,1,768]{2,0,1:T(8,128)(2,1)S(1)} collective-permute-done((bf16[34,1,768]{2,0,1:T(8,128)(2,1)S(1)}, bf16[34,1,768]{2,0,1:T(8,128)(2,1)S(1)}, u32[]{:S(2)}, u32[]{:S(2)}) %collective-permute-start.2) | collective-permute-done | bytes 52256 | tf_op jit(solution)/shard_map/ppermute | solution.py:26
  19.5 0.1 copy.16
  19.5 0.3 maximum_bitcast_fusion.side_ref
  19.8 0.2 broadcast_in_dim.9.live_ref
  20.0 0.0 copy-done.2
  20.0 0.0 copy-start.1
  20.0 2.2 %copy-done.1 = bf16[1024,2048]{1,0:T(8,128)(2,1)S(1)} copy-done((bf16[1024,2048]{1,0:T(8,128)(2,1)S(1)}, bf16[1024,2048]{1,0:T(8,128)(2,1)}, u32[]{:S(2)}) %copy-start.1) | copy-done | bytes 4194328
  22.2 0.0 copy-start.4
  22.2 1.4 %copy-done.4 = bf16[768,1024]{1,0:T(8,128)(2,1)S(1)} copy-done((bf16[768,1024]{1,0:T(8,128)(2,1)S(1)}, bf16[768,1024]{1,0:T(8,128)(2,1)}, u32[]{:S(2)}) %copy-start.4) | copy-done | bytes 1572888
  23.6 0.0 copy-start.5
  23.6 1.1 %copy-done.5 = bf16[9,32,1024]{2,1,0:T(8,128)(2,1)S(1)} copy-done((bf16[9,32,1024]{2,1,0:T(8,128)(2,1)S(1)}, bf16[9,32,1024]{2,1,0:T(8,128)(2,1)}, u32[]{:S(2)}) %copy-start.5) | copy-done | bytes 589848
  24.7 0.0 copy-start.3
  24.7 33.9 %local_work.1 = (bf16[1024,1024]{1,0:T(8,128)(2,1)}, bf16[512,1024]{1,0:T(8,128)(2,1)S(1)}, f32[512,128]{1,0:T(8,128)S(1)}) custom-call(bf16[1024,768]{1,0:T(8,128)(2,1)S(1)} %bitcast.18, bf16[32,768]{1,0:T(8,128)(2,1)S(1)} %bitcast.22, bf16[32,768]{1,0:T(8,128)(2,1)S(1)} %bitcast.21, bf16[272,768]{1,0:T(8,128)(2,1)S(1)} %maximum_bitcast_fusion.side_ref, ...), custom_call_target="tpu_custom_call" | custom-call | tf_op jit(solution)/shard_map/local_work/pallas_call | solution.py:148
  58.6 0.0 copy-done.3
  58.6 29.2 %combine.1 = bf16[16,1024]{1,0:T(8,128)(2,1)S(1)} custom-call(bf16[4,4,2,16,1024]{4,3,2,1,0:T(8,128)(2,1)S(1)} %bitcast.19, f32[4,4,2,16,128]{4,3,2,1,0:T(8,128)S(1)} %bitcast.20, bf16[1024,1024]{1,0:T(8,128)(2,1)S(1)} %copy-done.3), custom_call_target="tpu_custom_call" | custom-call | tf_op jit(solution)/shard_map/combine/pallas_call | solution.py:312
  87.8 0.6 copy.21
  (11 shorter events, 0.1 us)
Async XLA Ops:
  0.6 9.1 %copy-start = (bf16[1024,1024]{1,0:T(8,128)(2,1)S(1)}, bf16[1024,1024]{1,0:T(8,128)(2,1)}, u32[]{:S(2)}) copy-start(bf16[1024,1024]{1,0:T(8,128)(2,1)} %param.13) | copy-start | bytes 6291460
  1.6 10.8 %collective-permute-start.1 = (bf16[1,32,768]{2,1,0:T(8,128)(2,1)S(1)}, bf16[1,32,768]{2,1,0:T(8,128)(2,1)S(1)}, u32[]{:S(2)}, u32[]{:S(2)}) collective-permute-start(bf16[1,32,768]{2,1,0:T(8,128)(2,1)S(1)} %get-tuple-element.10), channel_id=1, source_target_pairs={{8,0},{16,8},{24,16},{9,1},{17,9},{25,17},{10,2},{18,10},{26,18},{... | collective-permute-start | bytes 147464 | tf_op jit(solution)/shard_map/ppermute | solution.py:26
  2.9 9.5 %collective-permute-start = (bf16[1,32,768]{2,1,0:T(8,128)(2,1)S(1)}, bf16[1,32,768]{2,1,0:T(8,128)(2,1)S(1)}, u32[]{:S(2)}, u32[]{:S(2)}) collective-permute-start(bf16[1,32,768]{2,1,0:T(8,128)(2,1)S(1)} %get-tuple-element.11), channel_id=1, source_target_pairs={{0,8},{8,16},{16,24},{1,9},{9,17},{17,25},{2,10},{10,18},{18,26},{... | collective-permute-start | bytes 147464 | tf_op jit(solution)/shard_map/ppermute | solution.py:26
  9.7 2.5 %copy-start.6 = (s32[32,32]{1,0:T(8,128)S(1)}, s32[32,32]{1,0:T(8,128)}, u32[]{:S(2)}) copy-start(s32[32,32]{1,0:T(8,128)} %param.9) | copy-start | bytes 12292
  12.3 7.7 %copy-start.2 = (bf16[32,32,768]{2,1,0:T(8,128)(2,1)S(1)}, bf16[32,32,768]{2,1,0:T(8,128)(2,1)}, u32[]{:S(2)}) copy-start(bf16[32,32,768]{2,1,0:T(8,128)(2,1)} %param.8) | copy-start | bytes 4718596
  12.5 2.9 %collective-permute-start.3 = (bf16[34,1,768]{2,0,1:T(8,128)(2,1)S(1)}, bf16[34,1,768]{2,0,1:T(8,128)(2,1)S(1)}, u32[]{:S(2)}, u32[]{:S(2)}) collective-permute-start(bf16[34,1,768]{2,0,1:T(8,128)(2,1)S(1)} %pad_maximum_fusion.1), channel_id=1, source_target_pairs={{0,1},{1,2},{2,3},{3,4},{4,5},{5,6},{6,7},{8,9},{9,10},{10,11},{11... | collective-permute-start | bytes 156680 | tf_op jit(solution)/shard_map/ppermute | solution.py:26
  14.2 5.3 %collective-permute-start.2 = (bf16[34,1,768]{2,0,1:T(8,128)(2,1)S(1)}, bf16[34,1,768]{2,0,1:T(8,128)(2,1)S(1)}, u32[]{:S(2)}, u32[]{:S(2)}) collective-permute-start(bf16[34,1,768]{2,0,1:T(8,128)(2,1)S(1)} %pad_maximum_fusion), channel_id=1, source_target_pairs={{1,0},{2,1},{3,2},{4,3},{5,4},{6,5},{7,6},{9,8},{10,9},{11,10},{12... | collective-permute-start | bytes 156680 | tf_op jit(solution)/shard_map/ppermute | solution.py:26
  20.0 2.2 %copy-start.1 = (bf16[1024,2048]{1,0:T(8,128)(2,1)S(1)}, bf16[1024,2048]{1,0:T(8,128)(2,1)}, u32[]{:S(2)}) copy-start(bf16[1024,2048]{1,0:T(8,128)(2,1)} %kv_ref.1) | copy-start | bytes 12582916
  22.2 1.4 %copy-start.4 = (bf16[768,1024]{1,0:T(8,128)(2,1)S(1)}, bf16[768,1024]{1,0:T(8,128)(2,1)}, u32[]{:S(2)}) copy-start(bf16[768,1024]{1,0:T(8,128)(2,1)} %patch_ref.1) | copy-start | bytes 4718596
  23.6 1.1 %copy-start.5 = (bf16[9,32,1024]{2,1,0:T(8,128)(2,1)S(1)}, bf16[9,32,1024]{2,1,0:T(8,128)(2,1)}, u32[]{:S(2)}) copy-start(bf16[9,32,1024]{2,1,0:T(8,128)(2,1)} %conv_ref.1) | copy-start | bytes 1769476
  24.7 33.9 %copy-start.3 = (bf16[1024,1024]{1,0:T(8,128)(2,1)S(1)}, bf16[1024,1024]{1,0:T(8,128)(2,1)}, u32[]{:S(2)}) copy-start(bf16[1024,1024]{1,0:T(8,128)(2,1)} %weight_hbm.1) | copy-start | bytes 6291460

commit v2 on v1

--- a/solution.py
+++ b/solution.py
@@ -11,27 +11,36 @@
 BLOCK = 256
 LANES = 128
 PAD = 8
+CORNER = 16
 F32 = jnp.float32
 BF16 = jnp.bfloat16
 LOW = -1e30
+MESH = pl.DeviceIdType.MESH
 
 
 def dot(a, b):
     return jnp.dot(a, b, preferred_element_type=F32)
 
 
-def shifted(cells, axis, step):
-    count = lax.axis_size(axis)
-    pairs = [(i, i + step) for i in range(count) if 0 <= i + step < count]
-    return lax.ppermute(cells, axis, pairs)
-
-
 def core(
     tile_rows, tile_cols, heads,
-    main_ref, top_ref, bottom_ref, side_ref, live_ref, patch_ref, conv_ref, kv_ref, query_ref,
-    features_ref, part_ref, stat_ref,
-    wide_ref, taps_ref, summed_ref, keys_ref,
+    top_ref, bottom_ref, left_ref, right_ref, live_ref,
+    main_hbm, patch_hbm, conv_hbm, latent_hbm, weight_hbm, kv_hbm,
+    part_ref, stat_ref, features_hbm,
+    main_ref, patch_ref, conv_ref, latent_ref, weight_ref, kv_ref,
+    wide_ref, taps_ref, summed_ref, keys_ref, query_ref, features_ref, load_sem,
 ):
+    loads = [
+        pltpu.make_async_copy(source, target, load_sem.at[number])
+        for number, (source, target) in enumerate(
+            (
+                (main_hbm, main_ref), (patch_hbm, patch_ref), (conv_hbm, conv_ref),
+                (latent_hbm, latent_ref), (weight_hbm, weight_ref), (kv_hbm, kv_ref),
+            )
+        )
+    ]
+    for load in loads:
+        load.start()
     tokens = tile_rows * tile_cols
     channels = patch_ref.shape[1]
     group = conv_ref.shape[1]
@@ -41,15 +50,35 @@
         lax.broadcasted_iota(jnp.int32, (BLOCK, BLOCK), 0) // group
         == lax.broadcasted_iota(jnp.int32, (BLOCK, BLOCK), 1) // group
     )
+    side_slot = lax.broadcasted_iota(jnp.int32, (rows_ext, PAD, BLOCK), 1)
+    tall = (1, PAD, BLOCK)
+
+    def border(values, upper, lower):
+        return (
+            jnp.broadcast_to(values[upper : upper + 1][:, None, :], tall),
+            jnp.broadcast_to(values[:tile_rows][:, None, :], (tile_rows, PAD, BLOCK)),
+            jnp.broadcast_to(values[lower : lower + 1][:, None, :], tall),
+        )
+
+    for load in loads[:3]:
+        load.wait()
     for block in range(channels // BLOCK):
         lanes = slice(block * BLOCK, (block + 1) * BLOCK)
         patch = patch_ref[:, lanes]
         inner = jnp.concatenate(
             [dot(top_ref[...], patch), dot(main_ref[...], patch), dot(bottom_ref[...], patch)], 0
         )
-        side = dot(side_ref[...], patch)
+        upper, middle, lower = border(
+            dot(left_ref[...], patch), tile_rows + CORNER - 1, tile_rows + 2 * CORNER - 1
+        )
+        from_left = jnp.concatenate([middle, lower, upper], 0)
+        upper, middle, lower = border(
+            dot(right_ref[...], patch), tile_rows, tile_rows + CORNER
+        )
+        from_right = jnp.concatenate([upper, middle, lower], 0)
+        side = jnp.where(side_slot == PAD - 1, from_left, from_right)
         full = jnp.concatenate(
-            [inner.reshape(rows_ext, tile_cols, BLOCK), side.reshape(rows_ext, PAD, BLOCK)], 1
+            [inner.reshape(rows_ext, tile_cols, BLOCK), side], 1
         ).reshape(rows_ext * col_ext, BLOCK)
         for col_shift, amount in ((0, 1), (2, rows_ext * col_ext - 1)):
             moved = pltpu.roll(full, amount, 0).reshape(rows_ext, col_ext, BLOCK)
@@ -81,6 +110,19 @@
         return 0
 
     lax.fori_loop(0, tokens // chunk, normalise, 0)
+    store = pltpu.make_async_copy(features_ref, features_hbm, load_sem.at[len(loads)])
+    store.start()
+    head_dim = channels // heads
+    for load in loads[3:]:
+        load.wait()
+
+    def ask(step, _):
+        at = pl.ds(pl.multiple_of(step * BLOCK, BLOCK), BLOCK)
+        asked = dot(latent_ref[...], weight_ref[:, at]).astype(BF16).astype(F32)
+        query_ref[:, at] = (asked * head_dim ** -0.5).astype(BF16)
+        return 0
+
+    lax.fori_loop(0, channels // BLOCK, ask, 0)
 
     def project(step, _):
         at = pl.ds(pl.multiple_of(step * BLOCK, BLOCK), BLOCK)
@@ -90,7 +132,6 @@
     lax.fori_loop(0, keys_ref.shape[1] // BLOCK, project, 0)
 
     latent_count = query_ref.shape[0]
-    head_dim = channels // heads
     token_lane = lax.broadcasted_iota(jnp.int32, (tokens, LANES), 1)
     query_lane = lax.broadcasted_iota(jnp.int32, (latent_count, LANES), 1)
     token_low = token_lane < head_dim
@@ -136,39 +177,130 @@
         return 0
 
     lax.fori_loop(0, heads // 2, attend, 0)
-
-
-def local_work(pixels, top, bottom, side, live, patch_weight, conv_weight, kv_weight, queries):
+    store.wait()
+
+
+def local_work(borders, live, pixels, patch_weight, conv_weight, latents, query_weight, kv_weight):
     tile_rows, tile_cols, patch_in = pixels.shape
     channels = patch_weight.shape[1]
     tokens = tile_rows * tile_cols
-    latent_count = queries.shape[0]
+    latent_count = latents.shape[0]
     rows_ext = tile_rows + 2
     vmem = pl.BlockSpec(memory_space=pltpu.VMEM)
-    return pl.pallas_call(
+    leave = pl.BlockSpec(memory_space=pl.ANY)
+    loaded = (
+        pixels.reshape(tokens, patch_in), patch_weight, conv_weight, latents, query_weight, kv_weight,
+    )
+    part, stat, features = pl.pallas_call(
         functools.partial(core, tile_rows, tile_cols, HEADS),
         out_shape=(
-            jax.ShapeDtypeStruct((tokens, channels), BF16),
             jax.ShapeDtypeStruct((latent_count, channels), BF16),
             jax.ShapeDtypeStruct((latent_count, LANES), F32),
+            jax.ShapeDtypeStruct((tokens, channels), BF16),
         ),
-        in_specs=[vmem] * 9,
-        out_specs=(vmem, vmem, vmem),
-        scratch_shapes=[
+        in_specs=[vmem] * 5 + [leave] * len(loaded),
+        out_specs=(vmem, vmem, leave),
+        scratch_shapes=[pltpu.VMEM(array.shape, BF16) for array in loaded]
+        + [
             pltpu.VMEM((rows_ext * tile_cols, 3 * BLOCK), BF16),
             pltpu.VMEM((3, 3 * BLOCK, BLOCK), BF16),
             pltpu.VMEM((tokens, channels), F32),
             pltpu.VMEM((tokens, 2 * channels), BF16),
+            pltpu.VMEM((latent_count, channels), BF16),
+            pltpu.VMEM((tokens, channels), BF16),
+            pltpu.SemaphoreType.DMA((len(loaded) + 1,)),
         ],
-        compiler_params=pltpu.CompilerParams(vmem_limit_bytes=40 * 1024 * 1024),
+        compiler_params=pltpu.CompilerParams(vmem_limit_bytes=60 * 1024 * 1024),
         name="local_work",
-    )(
-        pixels.reshape(tokens, patch_in), top, bottom,
-        side.reshape(rows_ext * PAD, patch_in), live, patch_weight, conv_weight, kv_weight, queries,
-    )
-
-
-MESH = pl.DeviceIdType.MESH
+    )(*borders, live, *loaded)
+    return features, part, stat
+
+
+def greet(
+    pixels_ref, first_ref, last_ref,
+    top_ref, bottom_ref, left_ref, right_ref,
+    send_sem, recv_sem,
+):
+    tile_rows, tile_cols, _ = pixels_ref.shape
+    row_count, col_count = lax.axis_size("rows"), lax.axis_size("cols")
+    row, col = lax.axis_index("rows"), lax.axis_index("cols")
+    low, high = slice(0, CORNER), slice(tile_cols - CORNER, tile_cols)
+    column = slice(0, tile_rows)
+    above = slice(tile_rows, tile_rows + CORNER)
+    below = slice(tile_rows + CORNER, tile_rows + 2 * CORNER)
+    end = tile_rows - 1
+    moves = (
+        (1, 0, pixels_ref.at[end], top_ref),
+        (-1, 0, pixels_ref.at[0], bottom_ref),
+        (0, 1, last_ref, left_ref.at[column]),
+        (0, -1, first_ref, right_ref.at[column]),
+        (1, 1, pixels_ref.at[end, high], left_ref.at[above]),
+        (1, -1, pixels_ref.at[end, low], right_ref.at[above]),
+        (-1, 1, pixels_ref.at[0, high], left_ref.at[below]),
+        (-1, -1, pixels_ref.at[0, low], right_ref.at[below]),
+    )
+
+    def inside(down, across):
+        ok = None
+        for at, step, count in ((row, down, row_count), (col, across, col_count)):
+            if step:
+                here = at + step < count if step > 0 else at + step >= 0
+                ok = here if ok is None else jnp.logical_and(ok, here)
+        return ok
+
+    barrier = pltpu.get_barrier_semaphore()
+    for down, across, _, _ in moves:
+        @pl.when(inside(down, across))
+        def _(down=down, across=across):
+            pl.semaphore_signal(
+                barrier, inc=1, device_id=(row + down, col + across), device_id_type=MESH
+            )
+    tall = 1 + (row > 0).astype(jnp.int32) + (row < row_count - 1).astype(jnp.int32)
+    wide = 1 + (col > 0).astype(jnp.int32) + (col < col_count - 1).astype(jnp.int32)
+    pl.semaphore_wait(barrier, tall * wide - 1)
+
+    def make(number):
+        down, across, source, target = moves[number]
+        return pltpu.make_async_remote_copy(
+            src_ref=source, dst_ref=target,
+            send_sem=send_sem.at[number], recv_sem=recv_sem.at[number],
+            device_id=(row + down, col + across), device_id_type=MESH,
+        )
+
+    for number, (down, across, _, _) in enumerate(moves):
+        @pl.when(inside(down, across))
+        def _(number=number):
+            make(number).start()
+    for number, (down, across, _, target) in enumerate(moves):
+        @pl.when(inside(-down, -across))
+        def _(number=number):
+            make(number).wait_recv()
+
+        @pl.when(jnp.logical_not(inside(-down, -across)))
+        def _(target=target):
+            target[...] = jnp.zeros(target.shape, BF16)
+    for number, (down, across, _, _) in enumerate(moves):
+        @pl.when(inside(down, across))
+        def _(number=number):
+            make(number).wait_send()
+
+
+def borders_of(pixels):
+    tile_rows, tile_cols, patch_in = pixels.shape
+    vmem = pl.BlockSpec(memory_space=pltpu.VMEM)
+    flat = jax.ShapeDtypeStruct((tile_cols, patch_in), BF16)
+    tall = jax.ShapeDtypeStruct((tile_rows + 2 * CORNER, patch_in), BF16)
+    return pl.pallas_call(
+        greet,
+        out_shape=(flat, flat, tall, tall),
+        in_specs=[pl.BlockSpec(memory_space=pl.ANY), vmem, vmem],
+        out_specs=(vmem,) * 4,
+        scratch_shapes=[pltpu.SemaphoreType.DMA((8,)), pltpu.SemaphoreType.DMA((8,))],
+        compiler_params=pltpu.CompilerParams(
+            collective_id=2, has_side_effects=True, vmem_limit_bytes=60 * 1024 * 1024
+        ),
+        name="borders",
+    )(pixels, pixels[:, 0], pixels[:, -1])
 
 
 def spread(values, heads, head_dim, low):
@@ -333,24 +465,12 @@
 
 
 def shards(pixels, tissue, patch_weight, conv_weight, kv_weight, query_weight, out_weight, latents):
-    tile_rows, tile_cols, patch_in = pixels.shape
+    tile_rows, tile_cols, _ = pixels.shape
     channels = patch_weight.shape[1]
     tokens = tile_rows * tile_cols
-    head_dim = channels // HEADS
-    latent_count = latents.shape[0]
-    top = shifted(pixels[-1:], "rows", 1)
-    bottom = shifted(pixels[:1], "rows", -1)
-    first = jnp.concatenate([top[:, :1], pixels[:, :1], bottom[:, :1]], 0)
-    last = jnp.concatenate([top[:, -1:], pixels[:, -1:], bottom[:, -1:]], 0)
-    left = shifted(last, "cols", 1)
-    right = shifted(first, "cols", -1)
-    side = jnp.concatenate(
-        [right, jnp.zeros((tile_rows + 2, PAD - 2, patch_in), BF16), jnp.roll(left, -1, 0)], 1
-    )
-    queries = (dot(latents, query_weight).astype(BF16) * (head_dim ** -0.5)).astype(BF16)
     live = jnp.broadcast_to((tissue.reshape(tokens, 1) > 0).astype(BF16), (tokens, LANES))
     features, part, stat = local_work(
-        pixels, top[0], bottom[0], side, live, patch_weight, conv_weight, kv_weight, queries
+        borders_of(pixels), live, pixels, patch_weight, conv_weight, latents, query_weight, kv_weight
     )
     latents_out = combine(part, stat, out_weight)
     return (features.reshape(tile_rows, tile_cols, channels), latents_out)

time: 88.8 us -> 84 us (0.946)
  Pallas kernels: 63.1 us -> 76.6 us
  starting transfers between devices: 9.67 us -> 0 us
  waiting for transfers between devices: 3.85 us -> 0 us
  matrix products: 2.48 us -> 0 us
  local copies, waits for them, and re-layouts: 8.13 us -> 5.7 us
    pallas_call x0 -> x1, Pallas kernels: none -> 11.6 us  [borders_of(): pl.pallas_call(greet, out_shape=(flat, flat, tall, tall), in_specs=[pl.Bl...]
    ppermute x4 -> x0, starting transfers between devices: 9.67 us -> none  [shifted(): return lax.ppermute(cells, axis, pairs)]
    pallas_call x1, Pallas kernels: 33.9 us -> 38.7 us  [local_work(): pl.pallas_call(functools.partial(core, tile_rows, tile_cols, HEADS), out_...]
    ppermute x4 -> x0, waiting for transfers between devices: 3.85 us -> none  [shifted(): return lax.ppermute(cells, axis, pairs)]
    pallas_call x1, Pallas kernels: 29.2 us -> 26.4 us  [combine(): pl.pallas_call(functools.partial(exchange, HEADS), out_shape=jax.ShapeDty...]
    unnamed x17 -> x7, local copies, waits for them, and re-layouts: 5.31 us -> 2.79 us
    dot_general x1 -> x0, matrix products: 2.48 us -> none  [dot(): return jnp.dot(a, b, preferred_element_type=F32)]
    slice x6 -> x1, local copies, waits for them, and re-layouts: 2.3 us -> 1.27 us  [borders_of(): pixels[:, -1]]
  transfers between devices with their start and end apart: 4 -> 0, of which waited for: 1 -> 0; matrix products, arithmetic and copies ran while one was open for 5% -> 0% of each run, Pallas kernels for 0% -> 0%
where the time goes in v2:
time: 84 us; the launch traced here: 83.7 us
  Pallas kernels  76.6 us (91%)
  local copies, waits for them, and re-layouts  5.7 us (7%)
    pallas_call x1, Pallas kernels, local_work(): pl.pallas_call(functools.partial(core, tile_rows, tile_cols, HEADS), out_...  38.7 us
    pallas_call x1, Pallas kernels, combine(): pl.pallas_call(functools.partial(exchange, HEADS), out_shape=jax.ShapeDty...  26.4 us
    pallas_call x1, Pallas kernels, borders_of(): pl.pallas_call(greet, out_shape=(flat, flat, tall, tall), in_specs=[pl.Bl...  11.6 us
    unnamed x7, local copies, waits for them, and re-layouts  2.79 us

profile of v2, /device:TPU:0, one launch (start us, length us, event | category | flops | bytes accessed | tf_op | source)
XLA Modules:
  0.0 83.7 jit_solution(15268404269154258547)
XLA Ops:
  0.6 0.7 compare_convert_fusion
  1.4 0.1 reshape.34
  1.4 1.3 %fusion = (bf16[32,1,768]{2,1,0:T(2,128)(2,1)S(1)}, bf16[32,1,768]{2,1,0:T(2,128)(2,1)S(1)}) fusion(bf16[32,32,768]{2,1,0:T(8,128)(2,1)} %pixels_ref.1), kind=kLoop, calls=%fused_computation.3 | loop fusion | bytes 196608 | tf_op jit(solution)/shard_map/slice | solution.py:303
  2.7 0.6 copy_bitcast_fusion
  3.4 11.6 %borders.1 = (bf16[32,768]{1,0:T(8,128)(2,1)}, bf16[32,768]{1,0:T(8,128)(2,1)}, bf16[64,768]{1,0:T(8,128)(2,1)}, bf16[64,768]{1,0:T(8,128)(2,1)}) custom-call(bf16[32,32,768]{2,1,0:T(8,128)(2,1)} %pixels_ref.1, bf16[32,768]{1,0:T(8,128)(2,1)} %get-tuple-element.19.first_ref, bf16[32,768]{1,0:T(8,128)(2,1)} %get-tuple-element.18.last_ref), custom_call_target="tpu_custom_call" | custom-call | tf_op jit(solution)/shard_map/borders/pallas_call | solution.py:293
  14.9 0.9 %broadcast_in_dim.2.live_ref = bf16[1024,128]{1,0:T(8,128)(2,1)} broadcast(bf16[1024]{0:T(1024)(128)(2,1)S(1)} %reshape.34), dimensions={0} | broadcast | bytes 264192 | tf_op jit(solution)/shard_map/broadcast_in_dim | solution.py:471
  15.8 0.0 copy-start
  15.9 38.7 %local_work.1 = (bf16[512,1024]{1,0:T(8,128)(2,1)}, f32[512,128]{1,0:T(8,128)}, bf16[1024,1024]{1,0:T(8,128)(2,1)}) custom-call(bf16[32,768]{1,0:T(8,128)(2,1)} %get-tuple-element.9.top_ref, bf16[32,768]{1,0:T(8,128)(2,1)} %get-tuple-element.10.bottom_ref, bf16[64,768]{1,0:T(8,128)(2,1)} %get-tuple-element.11.left_ref, ...), custom_call_target="tpu_custom_call" | custom-call | tf_op jit(solution)/shard_map/local_work/pallas_call | solution.py:194
  54.5 0.0 copy-done
  54.5 0.0 copy-start.1
  54.5 1.2 %copy-done.1 = bf16[512,1024]{1,0:T(8,128)(2,1)S(1)} copy-done((bf16[512,1024]{1,0:T(8,128)(2,1)S(1)}, bf16[512,1024]{1,0:T(8,128)(2,1)}, u32[]{:S(2)}) %copy-start.1) | copy-done | bytes 1048600
  55.8 0.0 copy-start.2
  55.8 0.9 %copy-done.2 = f32[512,128]{1,0:T(8,128)S(1)} copy-done((f32[512,128]{1,0:T(8,128)S(1)}, f32[512,128]{1,0:T(8,128)}, u32[]{:S(2)}) %copy-start.2) | copy-done | bytes 262168
  56.7 26.4 %combine.1 = bf16[16,1024]{1,0:T(8,128)(2,1)S(1)} custom-call(bf16[4,4,2,16,1024]{4,3,2,1,0:T(8,128)(2,1)S(1)} %bitcast.8, f32[4,4,2,16,128]{4,3,2,1,0:T(8,128)S(1)} %bitcast.9, bf16[1024,1024]{1,0:T(8,128)(2,1)S(1)} %copy-done), custom_call_target="tpu_custom_call" | custom-call | tf_op jit(solution)/shard_map/combine/pallas_call | solution.py:444
  83.1 0.6 copy.17
Async XLA Ops:
  15.8 38.7 %copy-start = (bf16[1024,1024]{1,0:T(8,128)(2,1)S(1)}, bf16[1024,1024]{1,0:T(8,128)(2,1)}, u32[]{:S(2)}) copy-start(bf16[1024,1024]{1,0:T(8,128)(2,1)} %weight_hbm.3) | copy-start | bytes 6291460
  54.5 1.2 %copy-start.1 = (bf16[512,1024]{1,0:T(8,128)(2,1)S(1)}, bf16[512,1024]{1,0:T(8,128)(2,1)}, u32[]{:S(2)}) copy-start(bf16[512,1024]{1,0:T(8,128)(2,1)} %get-tuple-element.14) | copy-start | bytes 3145732
  55.8 0.9 %copy-start.2 = (f32[512,128]{1,0:T(8,128)S(1)}, f32[512,128]{1,0:T(8,128)}, u32[]{:S(2)}) copy-start(f32[512,128]{1,0:T(8,128)} %get-tuple-element.15) | copy-start | bytes 786436

commit v3 on v2

--- a/solution.py
+++ b/solution.py
@@ -25,17 +25,17 @@
 def core(
     tile_rows, tile_cols, heads,
     top_ref, bottom_ref, left_ref, right_ref, live_ref,
-    main_hbm, patch_hbm, conv_hbm, latent_hbm, weight_hbm, kv_hbm,
+    main_hbm, patch_hbm, conv_hbm, query_hbm, kv_hbm,
     part_ref, stat_ref, features_hbm,
-    main_ref, patch_ref, conv_ref, latent_ref, weight_ref, kv_ref,
-    wide_ref, taps_ref, summed_ref, keys_ref, query_ref, features_ref, load_sem,
+    main_ref, patch_ref, conv_ref, query_ref, kv_ref,
+    wide_ref, taps_ref, summed_ref, keys_ref, features_ref, load_sem,
 ):
     loads = [
         pltpu.make_async_copy(source, target, load_sem.at[number])
         for number, (source, target) in enumerate(
             (
                 (main_hbm, main_ref), (patch_hbm, patch_ref), (conv_hbm, conv_ref),
-                (latent_hbm, latent_ref), (weight_hbm, weight_ref), (kv_hbm, kv_ref),
+                (query_hbm, query_ref), (kv_hbm, kv_ref),
             )
         )
     ]
@@ -115,14 +115,6 @@
     head_dim = channels // heads
     for load in loads[3:]:
         load.wait()
-
-    def ask(step, _):
-        at = pl.ds(pl.multiple_of(step * BLOCK, BLOCK), BLOCK)
-        asked = dot(latent_ref[...], weight_ref[:, at]).astype(BF16).astype(F32)
-        query_ref[:, at] = (asked * head_dim ** -0.5).astype(BF16)
-        return 0
-
-    lax.fori_loop(0, channels // BLOCK, ask, 0)
 
     def project(step, _):
         at = pl.ds(pl.multiple_of(step * BLOCK, BLOCK), BLOCK)
@@ -180,16 +172,16 @@
     store.wait()
 
 
-def local_work(borders, live, pixels, patch_weight, conv_weight, latents, query_weight, kv_weight):
+def local_work(borders, queries, live, pixels, patch_weight, conv_weight, kv_weight):
     tile_rows, tile_cols, patch_in = pixels.shape
     channels = patch_weight.shape[1]
     tokens = tile_rows * tile_cols
-    latent_count = latents.shape[0]
+    latent_count = queries.shape[0]
     rows_ext = tile_rows + 2
     vmem = pl.BlockSpec(memory_space=pltpu.VMEM)
     leave = pl.BlockSpec(memory_space=pl.ANY)
     loaded = (
-        pixels.reshape(tokens, patch_in), patch_weight, conv_weight, latents, query_weight, kv_weight,
+        pixels.reshape(tokens, patch_in), patch_weight, conv_weight, queries, kv_weight,
     )
     part, stat, features = pl.pallas_call(
         functools.partial(core, tile_rows, tile_cols, HEADS),
@@ -206,7 +198,6 @@
             pltpu.VMEM((3, 3 * BLOCK, BLOCK), BF16),
             pltpu.VMEM((tokens, channels), F32),
             pltpu.VMEM((tokens, 2 * channels), BF16),
-            pltpu.VMEM((latent_count, channels), BF16),
             pltpu.VMEM((tokens, channels), BF16),
             pltpu.SemaphoreType.DMA((len(loaded) + 1,)),
         ],
@@ -217,10 +208,18 @@
 
 
 def greet(
-    pixels_ref, first_ref, last_ref,
-    top_ref, bottom_ref, left_ref, right_ref,
-    send_sem, recv_sem,
+    head_dim,
+    pixels_ref, first_ref, last_ref, latent_hbm, weight_hbm,
+    top_ref, bottom_ref, left_ref, right_ref, query_ref,
+    latent_ref, weight_ref, send_sem, recv_sem, load_sem,
 ):
+    loads = [
+        pltpu.make_async_copy(latent_hbm, latent_ref, load_sem.at[0]),
+        pltpu.make_async_copy(weight_hbm, weight_ref, load_sem.at[1]),
+    ]
+    for load in loads:
+        load.start()
+    channels = query_ref.shape[1]
     tile_rows, tile_cols, _ = pixels_ref.shape
     row_count, col_count = lax.axis_size("rows"), lax.axis_size("cols")
     row, col = lax.axis_index("rows"), lax.axis_index("cols")
@@ -271,6 +270,16 @@
         @pl.when(inside(down, across))
         def _(number=number):
             make(number).start()
+    for load in loads:
+        load.wait()
+
+    def ask(step, _):
+        at = pl.ds(pl.multiple_of(step * BLOCK, BLOCK), BLOCK)
+        asked = dot(latent_ref[...], weight_ref[:, at]).astype(BF16).astype(F32)
+        query_ref[:, at] = (asked * head_dim ** -0.5).astype(BF16)
+        return 0
+
+    lax.fori_loop(0, channels // BLOCK, ask, 0)
     for number, (down, across, _, target) in enumerate(moves):
         @pl.when(inside(-down, -across))
         def _(number=number):
@@ -285,22 +294,31 @@
             make(number).wait_send()
 
 
-def borders_of(pixels):
+def borders_of(pixels, latents, query_weight):
     tile_rows, tile_cols, patch_in = pixels.shape
     vmem = pl.BlockSpec(memory_space=pltpu.VMEM)
     flat = jax.ShapeDtypeStruct((tile_cols, patch_in), BF16)
     tall = jax.ShapeDtypeStruct((tile_rows + 2 * CORNER, patch_in), BF16)
-    return pl.pallas_call(
-        greet,
-        out_shape=(flat, flat, tall, tall),
-        in_specs=[pl.BlockSpec(memory_space=pl.ANY), vmem, vmem],
-        out_specs=(vmem,) * 4,
-        scratch_shapes=[pltpu.SemaphoreType.DMA((8,)), pltpu.SemaphoreType.DMA((8,))],
+    channels = query_weight.shape[1]
+    leave = pl.BlockSpec(memory_space=pl.ANY)
+    *borders, queries = pl.pallas_call(
+        functools.partial(greet, channels // HEADS),
+        out_shape=(flat, flat, tall, tall, jax.ShapeDtypeStruct((latents.shape[0], channels), BF16)),
+        in_specs=[leave, vmem, vmem, leave, leave],
+        out_specs=(vmem,) * 5,
+        scratch_shapes=[
+            pltpu.VMEM(latents.shape, BF16),
+            pltpu.VMEM(query_weight.shape, BF16),
+            pltpu.SemaphoreType.DMA((8,)),
+            pltpu.SemaphoreType.DMA((8,)),
+            pltpu.SemaphoreType.DMA((2,)),
+        ],
         compiler_params=pltpu.CompilerParams(
             collective_id=2, has_side_effects=True, vmem_limit_bytes=60 * 1024 * 1024
         ),
         name="borders",
-    )(pixels, pixels[:, 0], pixels[:, -1])
+    )(pixels, pixels[:, 0], pixels[:, -1], latents, query_weight)
+    return borders, queries
 
 
 def spread(values, heads, head_dim, low):
@@ -365,60 +383,60 @@
         copy.start()
         return copy
 
-    copies = [
-        send(part_ref.at[:, :, 1 - side], part_one, twin, 0),
-        send(stat_ref.at[:, :, 1 - side], stat_one, twin, 1),
-    ]
-    for copy in copies:
-        copy.wait()
-
-    def first(index, _):
-        a, b = lax.div(index, half), lax.rem(index, half)
+    row_order = [lax.rem(row + step, row_count) for step in range(1, row_count + 1)]
+    col_order = [lax.rem(slot + step, half) for step in range(1, half + 1)]
+    ones, twos, threes = [], [], []
+    for step, a in enumerate(row_order):
+        ones.append(
+            (
+                send(part_ref.at[a, :, 1 - side], part_one.at[a], twin, 2 * step),
+                send(stat_ref.at[a, :, 1 - side], stat_one.at[a], twin, 2 * step + 1),
+            )
+        )
+    number = 2 * row_count
+    for step, a in enumerate(row_order):
+        for copy in ones[step]:
+            copy.wait_recv()
+
+        def first(b, _, a=a):
+            columns, stat = blend(
+                [part_ref[a, b, side], part_one[a, b]], [stat_ref[a, b, side], stat_one[a, b]],
+                heads, head_dim,
+            )
+            for pair, column in enumerate(columns):
+                sum_one[a, b, :, pair * LANES : (pair + 1) * LANES] = column.astype(BF16)
+            tot_one[a, b] = stat
+            return 0
+
+        lax.fori_loop(0, half, first, 0)
+        if step < row_count - 1:
+            twos.append(send(sum_one.at[a], part_two.at[step], row_peers[step], number))
+            twos.append(send(tot_one.at[a], stat_two.at[step], row_peers[step], number + 1))
+            number += 2
+    for copy in twos:
+        copy.wait_recv()
+    for step, b in enumerate(col_order):
         columns, stat = blend(
-            [part_ref[a, b, side], part_one[a, b]], [stat_ref[a, b, side], stat_one[a, b]],
+            [sum_one[row, b]] + [part_two[other, b] for other in range(row_count - 1)],
+            [tot_one[row, b]] + [stat_two[other, b] for other in range(row_count - 1)],
             heads, head_dim,
         )
-        for pair, column in enumerate(columns):
-            sum_one[a, b, :, pair * LANES : (pair + 1) * LANES] = column.astype(BF16)
-        tot_one[a, b] = stat
-        return 0
-
-    lax.fori_loop(0, row_count * half, first, 0)
-
-    copies = []
-    for step, peer in enumerate(row_peers):
-        number = 2 + 2 * step
-        copies.append(send(sum_one.at[peer[0]], part_two.at[step], peer, number))
-        copies.append(send(tot_one.at[peer[0]], stat_two.at[step], peer, number + 1))
-    for copy in copies:
-        copy.wait()
-
-    def second(b, _):
-        columns, stat = blend(
-            [sum_one[row, b]] + [part_two[step, b] for step in range(row_count - 1)],
-            [tot_one[row, b]] + [stat_two[step, b] for step in range(row_count - 1)],
-            heads, head_dim,
-        )
-        for pair, column in enumerate(columns):
-            sum_two[b, :, pair * LANES : (pair + 1) * LANES] = column.astype(BF16)
-        tot_two[b] = stat
-        return 0
-
-    lax.fori_loop(0, half, second, 0)
-
-    copies = []
-    for step, peer in enumerate(col_peers):
-        number = 2 * row_count + 2 * step
-        where = lax.rem(slot + step + 1, half)
-        copies.append(send(sum_two.at[where], part_three.at[step], peer, number))
-        copies.append(send(tot_two.at[where], stat_three.at[step], peer, number + 1))
-    for copy in copies:
-        copy.wait()
+        if step < half - 1:
+            for pair, column in enumerate(columns):
+                sum_two[b, :, pair * LANES : (pair + 1) * LANES] = column.astype(BF16)
+            tot_two[b] = stat
+            threes.append(send(sum_two.at[b], part_three.at[step], col_peers[step], number))
+            threes.append(send(tot_two.at[b], stat_three.at[step], col_peers[step], number + 1))
+            number += 2
+    for copy in threes:
+        copy.wait_recv()
     columns, _ = blend(
-        [sum_two[slot]] + [part_three[step] for step in range(half - 1)],
-        [tot_two[slot]] + [stat_three[step] for step in range(half - 1)],
+        [jnp.concatenate(columns, 1)] + [part_three[step] for step in range(half - 1)],
+        [stat] + [stat_three[step] for step in range(half - 1)],
         heads, head_dim,
     )
+    for copy in [copy for both in ones for copy in both] + twos + threes:
+        copy.wait_send()
     attended = jnp.concatenate(columns, 1)
     mean = jnp.sum(attended * attended, axis=-1, keepdims=True) * (1.0 / channels)
     normed = (attended * lax.rsqrt(mean + 1e-06)).astype(BF16)
@@ -434,7 +452,7 @@
     part = part.reshape(row_count, half, 2, own, channels)
     stat = stat.reshape(row_count, half, 2, own, LANES)
     vmem = pl.BlockSpec(memory_space=pltpu.VMEM)
-    copies = 2 + 2 * (row_count - 1) + 2 * (half - 1)
+    copies = 2 * (2 * row_count - 1) + 2 * (half - 1)
 
     def pairs(*extent):
         return [
@@ -469,8 +487,9 @@
     channels = patch_weight.shape[1]
     tokens = tile_rows * tile_cols
     live = jnp.broadcast_to((tissue.reshape(tokens, 1) > 0).astype(BF16), (tokens, LANES))
+    borders, queries = borders_of(pixels, latents, query_weight)
     features, part, stat = local_work(
-        borders_of(pixels), live, pixels, patch_weight, conv_weight, latents, query_weight, kv_weight
+        borders, queries, live, pixels, patch_weight, conv_weight, kv_weight
     )
     latents_out = combine(part, stat, out_weight)
     return (features.reshape(tile_rows, tile_cols, channels), latents_out)

time: 84 us -> 77.9 us (0.927)
  Pallas kernels: 76.6 us -> 70.4 us
    pallas_call x1, Pallas kernels: 26.4 us -> 21.5 us  [combine(): pl.pallas_call(functools.partial(exchange, HEADS), out_shape=jax.ShapeDty...]
    pallas_call x1, Pallas kernels: 38.7 us -> 36.9 us  [local_work(): pl.pallas_call(functools.partial(core, tile_rows, tile_cols, HEADS), out_...]
where the time goes in v3:
time: 77.9 us; the launch traced here: 77.5 us
  Pallas kernels  70.4 us (90%)
  local copies, waits for them, and re-layouts  5.7 us (7%)
    pallas_call x1, Pallas kernels, local_work(): pl.pallas_call(functools.partial(core, tile_rows, tile_cols, HEADS), out_...  36.9 us
    pallas_call x1, Pallas kernels, combine(): pl.pallas_call(functools.partial(exchange, HEADS), out_shape=jax.ShapeDty...  21.5 us
    pallas_call x1, Pallas kernels, borders_of(): pl.pallas_call(functools.partial(greet, channels // HEADS), out_shape=(fl...  12 us
    unnamed x7, local copies, waits for them, and re-layouts  2.79 us

profile of v3, /device:TPU:0, one launch (start us, length us, event | category | flops | bytes accessed | tf_op | source)
XLA Modules:
  0.0 77.5 jit_solution(18121425705523116690)
XLA Ops:
  0.6 0.7 compare_convert_fusion
  1.4 0.1 reshape.34
  1.4 1.3 %fusion = (bf16[32,1,768]{2,1,0:T(2,128)(2,1)S(1)}, bf16[32,1,768]{2,1,0:T(2,128)(2,1)S(1)}) fusion(bf16[32,32,768]{2,1,0:T(8,128)(2,1)} %pixels_ref.1), kind=kLoop, calls=%fused_computation.3 | loop fusion | bytes 196608 | tf_op jit(solution)/shard_map/slice | solution.py:320
  2.7 0.6 copy_bitcast_fusion
  3.4 0.9 %broadcast_in_dim.2.live_ref = bf16[1024,128]{1,0:T(8,128)(2,1)} broadcast(bf16[1024]{0:T(1024)(128)(2,1)S(1)} %reshape.34), dimensions={0} | broadcast | bytes 264192 | tf_op jit(solution)/shard_map/broadcast_in_dim | solution.py:489
  4.3 12.0 %borders.1 = (bf16[32,768]{1,0:T(8,128)(2,1)}, bf16[32,768]{1,0:T(8,128)(2,1)}, bf16[64,768]{1,0:T(8,128)(2,1)}, bf16[64,768]{1,0:T(8,128)(2,1)}, bf16[512,1024]{1,0:T(8,128)(2,1)}) custom-call(bf16[32,32,768]{2,1,0:T(8,128)(2,1)} %pixels_ref.1, bf16[32,768]{1,0:T(8,128)(2,1)} %get-tuple-element.21.first_ref, bf16[32,768]{1,0:T(8,128)(2,1)} %get-tuple-element.20.last_ref, ...), custom_call_target="tpu_custom_call" | custom-call | tf_op jit(solution)/shard_map/borders/pallas_call | solution.py:304
  16.3 0.0 copy-start
  16.3 36.9 %local_work.1 = (bf16[512,1024]{1,0:T(8,128)(2,1)}, f32[512,128]{1,0:T(8,128)}, bf16[1024,1024]{1,0:T(8,128)(2,1)}) custom-call(bf16[32,768]{1,0:T(8,128)(2,1)} %get-tuple-element.10.top_ref, bf16[32,768]{1,0:T(8,128)(2,1)} %get-tuple-element.11.bottom_ref, bf16[64,768]{1,0:T(8,128)(2,1)} %get-tuple-element.12.left_ref, ...), custom_call_target="tpu_custom_call" | custom-call | tf_op jit(solution)/shard_map/local_work/pallas_call | solution.py:186
  53.2 0.0 copy-done
  53.2 0.0 copy-start.1
  53.2 1.2 %copy-done.1 = bf16[512,1024]{1,0:T(8,128)(2,1)S(1)} copy-done((bf16[512,1024]{1,0:T(8,128)(2,1)S(1)}, bf16[512,1024]{1,0:T(8,128)(2,1)}, u32[]{:S(2)}) %copy-start.1) | copy-done | bytes 1048600
  54.4 0.0 copy-start.2
  54.4 0.9 %copy-done.2 = f32[512,128]{1,0:T(8,128)S(1)} copy-done((f32[512,128]{1,0:T(8,128)S(1)}, f32[512,128]{1,0:T(8,128)}, u32[]{:S(2)}) %copy-start.2) | copy-done | bytes 262168
  55.4 21.5 %combine.1 = bf16[16,1024]{1,0:T(8,128)(2,1)S(1)} custom-call(bf16[4,4,2,16,1024]{4,3,2,1,0:T(8,128)(2,1)S(1)} %bitcast.8, f32[4,4,2,16,128]{4,3,2,1,0:T(8,128)S(1)} %bitcast.9, bf16[1024,1024]{1,0:T(8,128)(2,1)S(1)} %copy-done), custom_call_target="tpu_custom_call" | custom-call | tf_op jit(solution)/shard_map/combine/pallas_call | solution.py:462
  76.9 0.6 copy.17
Async XLA Ops:
  16.3 36.9 %copy-start = (bf16[1024,1024]{1,0:T(8,128)(2,1)S(1)}, bf16[1024,1024]{1,0:T(8,128)(2,1)}, u32[]{:S(2)}) copy-start(bf16[1024,1024]{1,0:T(8,128)(2,1)} %weight_hbm.3) | copy-start | bytes 6291460
  53.2 1.2 %copy-start.1 = (bf16[512,1024]{1,0:T(8,128)(2,1)S(1)}, bf16[512,1024]{1,0:T(8,128)(2,1)}, u32[]{:S(2)}) copy-start(bf16[512,1024]{1,0:T(8,128)(2,1)} %get-tuple-element.16) | copy-start | bytes 3145732
  54.4 0.9 %copy-start.2 = (f32[512,128]{1,0:T(8,128)S(1)}, f32[512,128]{1,0:T(8,128)}, u32[]{:S(2)}) copy-start(f32[512,128]{1,0:T(8,128)} %get-tuple-element.17) | copy-start | bytes 786436

commit v4 on v3

--- a/solution.py
+++ b/solution.py
@@ -355,7 +355,7 @@
     part_ref, stat_ref, weight_hbm,
     out_ref,
     part_one, stat_one, sum_one, tot_one, part_two, stat_two, sum_two, tot_two,
-    part_three, stat_three, weight_ref, send_sem, recv_sem, load_sem,
+    part_three, stat_three, part_own, stat_own, weight_ref, send_sem, recv_sem, load_sem,
 ):
     row_count, half, _, own, channels = part_ref.shape
     head_dim = channels // heads
@@ -363,8 +363,13 @@
     col = lax.axis_index("cols")
     side = lax.rem(col, 2)
     slot = lax.div(col, 2)
-    load = pltpu.make_async_copy(weight_hbm, weight_ref, load_sem)
-    load.start()
+    mine = [
+        pltpu.make_async_copy(part_ref.at[:, :, side], part_own, load_sem.at[0]),
+        pltpu.make_async_copy(stat_ref.at[:, :, side], stat_own, load_sem.at[1]),
+    ]
+    load = pltpu.make_async_copy(weight_hbm, weight_ref, load_sem.at[2])
+    for copy in mine:
+        copy.start()
 
     twin = (row, slot * 2 + (1 - side))
     row_peers = [(lax.rem(row + step, row_count), col) for step in range(1, row_count)]
@@ -393,6 +398,9 @@
                 send(stat_ref.at[a, :, 1 - side], stat_one.at[a], twin, 2 * step + 1),
             )
         )
+    load.start()
+    for copy in mine:
+        copy.wait()
     number = 2 * row_count
     for step, a in enumerate(row_order):
         for copy in ones[step]:
@@ -400,7 +408,7 @@
 
         def first(b, _, a=a):
             columns, stat = blend(
-                [part_ref[a, b, side], part_one[a, b]], [stat_ref[a, b, side], stat_one[a, b]],
+                [part_own[a, b], part_one[a, b]], [stat_own[a, b], stat_one[a, b]],
                 heads, head_dim,
             )
             for pair, column in enumerate(columns):
@@ -462,21 +470,22 @@
     return pl.pallas_call(
         functools.partial(exchange, HEADS),
         out_shape=jax.ShapeDtypeStruct((own, out_weight.shape[1]), BF16),
-        in_specs=[vmem, vmem, pl.BlockSpec(memory_space=pl.ANY)],
+        in_specs=[pl.BlockSpec(memory_space=pl.ANY)] * 3,
         out_specs=vmem,
         scratch_shapes=pairs(row_count, half)
         + pairs(row_count, half)
         + pairs(row_count - 1, half)
         + pairs(half)
         + pairs(half - 1)
+        + pairs(row_count, half)
         + [
             pltpu.VMEM(out_weight.shape, BF16),
             pltpu.SemaphoreType.DMA((copies,)),
             pltpu.SemaphoreType.DMA((copies,)),
-            pltpu.SemaphoreType.DMA,
+            pltpu.SemaphoreType.DMA((3,)),
         ],
         compiler_params=pltpu.CompilerParams(
-            collective_id=1, has_side_effects=True, vmem_limit_bytes=24 * 1024 * 1024
+            collective_id=1, has_side_effects=True, vmem_limit_bytes=60 * 1024 * 1024
         ),
         name="combine",
     )(part, stat, out_weight)

time: 77.9 us -> 76.9 us (0.987)
  local copies, waits for them, and re-layouts: 5.7 us -> 4.31 us
    unnamed x7 -> x1, local copies, waits for them, and re-layouts: 2.79 us -> 1.38 us
where the time goes in v4:
time: 76.9 us; the launch traced here: 76.6 us
  Pallas kernels  70.9 us (92%)
  local copies, waits for them, and re-layouts  4.31 us (6%)
    pallas_call x1, Pallas kernels, local_work(): pl.pallas_call(functools.partial(core, tile_rows, tile_cols, HEADS), out_...  36.7 us
    pallas_call x1, Pallas kernels, combine(): pl.pallas_call(functools.partial(exchange, HEADS), out_shape=jax.ShapeDty...  22.2 us
    pallas_call x1, Pallas kernels, borders_of(): pl.pallas_call(functools.partial(greet, channels // HEADS), out_shape=(fl...  12 us

profile of v4, /device:TPU:0, one launch (start us, length us, event | category | flops | bytes accessed | tf_op | source)
XLA Modules:
  0.0 76.6 jit_solution(6655193306085128594)
XLA Ops:
  0.6 0.7 compare_convert_fusion
  1.4 0.1 reshape.34
  1.4 1.3 %fusion = (bf16[32,1,768]{2,1,0:T(2,128)(2,1)S(1)}, bf16[32,1,768]{2,1,0:T(2,128)(2,1)S(1)}) fusion(bf16[32,32,768]{2,1,0:T(8,128)(2,1)} %pixels_ref.1), kind=kLoop, calls=%fused_computation.3 | loop fusion | bytes 196608 | tf_op jit(solution)/shard_map/slice | solution.py:320
  2.7 0.6 copy_bitcast_fusion
  3.4 0.9 %broadcast_in_dim.2.live_ref = bf16[1024,128]{1,0:T(8,128)(2,1)} broadcast(bf16[1024]{0:T(1024)(128)(2,1)S(1)} %reshape.34), dimensions={0} | broadcast | bytes 264192 | tf_op jit(solution)/shard_map/broadcast_in_dim | solution.py:498
  4.3 12.0 %borders.1 = (bf16[32,768]{1,0:T(8,128)(2,1)}, bf16[32,768]{1,0:T(8,128)(2,1)}, bf16[64,768]{1,0:T(8,128)(2,1)}, bf16[64,768]{1,0:T(8,128)(2,1)}, bf16[512,1024]{1,0:T(8,128)(2,1)}) custom-call(bf16[32,32,768]{2,1,0:T(8,128)(2,1)} %pixels_ref.1, bf16[32,768]{1,0:T(8,128)(2,1)} %get-tuple-element.21.first_ref, bf16[32,768]{1,0:T(8,128)(2,1)} %get-tuple-element.20.last_ref, ...), custom_call_target="tpu_custom_call" | custom-call | tf_op jit(solution)/shard_map/borders/pallas_call | solution.py:304
  16.3 36.7 %local_work.1 = (bf16[512,1024]{1,0:T(8,128)(2,1)}, f32[512,128]{1,0:T(8,128)}, bf16[1024,1024]{1,0:T(8,128)(2,1)}) custom-call(bf16[32,768]{1,0:T(8,128)(2,1)} %get-tuple-element.10.top_ref, bf16[32,768]{1,0:T(8,128)(2,1)} %get-tuple-element.11.bottom_ref, bf16[64,768]{1,0:T(8,128)(2,1)} %get-tuple-element.12.left_ref, ...), custom_call_target="tpu_custom_call" | custom-call | tf_op jit(solution)/shard_map/local_work/pallas_call | solution.py:186
  53.0 22.2 %combine.1 = bf16[16,1024]{1,0:T(8,128)(2,1)} custom-call(bf16[4,4,2,16,1024]{4,3,2,1,0:T(8,128)(2,1)} %bitcast.9, f32[4,4,2,16,128]{4,3,2,1,0:T(8,128)} %bitcast.10, bf16[1024,1024]{1,0:T(8,128)(2,1)} %weight_hbm.3), custom_call_target="tpu_custom_call" | custom-call | tf_op jit(solution)/shard_map/combine/pallas_call | solution.py:470
  75.2 1.4 %copy.17 = bf16[16,1024]{1,0:T(8,128)(2,1)} copy(bf16[16,1024]{1,0:T(8,128)(2,1)} %combine.1) | data formatting | bytes 65536
